TPU v7x, 512 devices: a whole 4x8x8 slice. The times are simulated.
512 devices in a mesh: req: 32 (over y, x), exp: 16 (over z, core).
Axes of the slice: x: 4, y: 8, z: 8, core: 2. Of those that a mesh axis runs over, the one named last changes fastest.
Arguments:
- resid_in: bfloat16 [4096, 3584], P(('req', 'exp')), may hold values from -6 to 6
- queries: bfloat16 [4096, 3584], P(('req', 'exp')), may hold values from -40 to 40
- fresh_kv: bfloat16 [4096, 1024], P(('req', 'exp')), may hold values from -6 to 6
- kv_pool: bfloat16 [32, 16, 32, 16, 1024], P('req', 'exp'), may hold values from -6 to 6
- block_table: int32 [2048, 8], P(('req', 'exp')), may hold values from 0 to 31, as said below
- lengths: int32 [2048], P(('req', 'exp')), may hold values from 1 to 128, as said below
- mig_source: int32 [32, 16, 2, 4], P('req', 'exp'), may hold values from 0 to 31, as said below
- mig_target: int32 [32, 16, 2, 4], P('req', 'exp'), may hold values from 0 to 31, as said below
- expert_ids: int32 [4096, 8], P('req'), may hold values from 0 to 63, all different within a row; in each aligned block of 128 rows (0 to 127, 128 to 255, ...) at most 24 rows name the same one
- gate_values: float32 [4096, 8], P('req'), may hold values from 0.2 to 1
- norm_gain: bfloat16 [3584], replicated, may hold values from 0.5 to 1.5
- w_in: bfloat16 [16, 32, 3584, 256], P('exp', 'req'), may hold values from -0.09375 to 0.09375
- w_out: bfloat16 [16, 32, 256, 3584], P('exp', 'req'), may hold values from -0.125 to 0.125
Outputs:
- mixed: bfloat16 [4096, 3584], P(('req', 'exp'))
Inputs may be any that keep to these rules, and one draw needn't show every extreme that they name: `block_table`: the entries of the 4 rows of one device are distinct pages of that device's pool. `lengths`: A request that arrives by migration has more than (3) * 16 cached positions. `mig_target`: on every device exactly one request arrives from req index - 1 and one from index + 1 (around the loop); [r, e, 0, i] is the page that takes page i of the request from index - 1, [r, e, 1, i] of the one from index + 1; they are the first 4 entries of that request's block-table row. `mig_source`: [r, e, 0, i] is the pool page sent as page i to index + 1, [r, e, 1, i] to index - 1; the 8 pages of a device are distinct and belong to no request that stays on it. `expert_ids`: each row names 8 different experts; among the 128 tokens of one index of req no expert is named by more than 24 rows.
All inputs are finite; a program needn't handle non-finite values.
Results may differ from a plain program's by a relative error of at most 0.012.
Values may be sent and summed in bfloat16 or wider, within the bound.
A program may use at most 64 MiB of HBM per device.

v0:
```python
import jax
import jax.numpy as jnp
from jax import lax
from jax.sharding import PartitionSpec as P

HEADS = 28
KV_HEADS = 4
HEAD_DIM = 128
EXP_DEV = 4
CAP = 24
neg_big = -1e30
norm_eps = 1e-06


def with_halo(block, sides, width):
    for axis, dim in sides:
        count = lax.axis_size(axis)
        forward = [(i, i + 1) for i in range(count - 1)]
        forward.append((count - 1, 0))
        backward = [(target, source) for source, target in forward]
        low = lax.ppermute(
            lax.slice_in_dim(block, block.shape[dim] - width, None, axis=dim), axis, forward
        )
        high = lax.ppermute(lax.slice_in_dim(block, 0, width, axis=dim), axis, backward)
        block = jnp.concatenate([low, block, high], axis=dim)
    return block


def partial_attention(query_grid, key_rows, visible):
    request_count = key_rows.shape[0]
    span = key_rows.shape[1]
    key_width = KV_HEADS * HEAD_DIM
    key_part = key_rows[:, :, :key_width].reshape(request_count, span, KV_HEADS, HEAD_DIM)
    value_part = (
        key_rows[:, :, key_width:]
        .reshape(request_count, span, KV_HEADS, HEAD_DIM)
        .astype(jnp.float32)
    )
    scores = jnp.einsum(
        "rdkgh,rpkh->rdkgp", query_grid, key_part, preferred_element_type=jnp.float32
    ) * HEAD_DIM ** (-0.5)
    live = visible[:, :, None, None, :]
    scores = jnp.where(live, scores, neg_big)
    highest = jnp.max(scores, axis=-1)
    weights = jnp.where(live, jnp.exp(scores - highest[..., None]), 0.0)
    weight_sum = jnp.sum(weights, axis=-1)
    summed = jnp.einsum("rdkgp,rpkh->rdkgh", weights, value_part, precision=lax.Precision.HIGHEST)
    return (highest, weight_sum, summed)


def body(
    resid_in,
    queries,
    fresh_kv,
    kv_pool,
    block_table,
    lengths,
    mig_source,
    mig_target,
    expert_ids,
    gate_values,
    norm_gain,
    w_in,
    w_out,
):
    request_count = block_table.shape[0]
    table_width = block_table.shape[1]
    page_tokens = kv_pool.shape[3]
    kv_width = kv_pool.shape[4]
    cache_span = table_width * page_tokens
    token_count = resid_in.shape[0]
    draft_count = token_count // request_count
    model_width = resid_in.shape[1]
    moved = mig_source.shape[3]
    pool_pages = kv_pool[0, 0]
    sources = mig_source[0, 0]
    target_pairs = mig_target[0, 0]
    outgoing = jnp.concatenate([pool_pages[sources[1]], pool_pages[sources[0]]], axis=0)
    targets = jnp.concatenate([target_pairs[0], target_pairs[1]], axis=0)
    extended = with_halo(outgoing, (("req", 0),), moved)
    arrivals = jnp.concatenate([extended[:moved], extended[-moved:]], axis=0)
    query_grid = queries.reshape(request_count, draft_count, KV_HEADS, HEADS // KV_HEADS, HEAD_DIM)
    fresh_rows = fresh_kv.reshape(request_count, draft_count, kv_width)
    position = jnp.arange(cache_span)
    cache_visible = jnp.broadcast_to(
        position[None, None, :] < lengths[:, None, None], (request_count, draft_count, cache_span)
    )
    draft_index = jnp.arange(draft_count)
    draft_visible = jnp.broadcast_to(
        draft_index[None, :] <= draft_index[:, None], (request_count, draft_count, draft_count)
    )
    pool_after = pool_pages.at[targets].set(arrivals)
    cache_rows = pool_after[block_table].reshape(request_count, cache_span, kv_width)
    parts = partial_attention(
        query_grid,
        jnp.concatenate([cache_rows, fresh_rows], axis=1),
        jnp.concatenate([cache_visible, draft_visible], axis=2),
    )
    attention = (parts[2] / parts[1][..., None]).reshape(token_count, model_width)
    residual = resid_in.astype(jnp.float32) + attention
    inv_rms = lax.rsqrt(jnp.mean(residual * residual, axis=1, keepdims=True) + norm_eps)
    normed = (residual * inv_rms * norm_gain.astype(jnp.float32)).astype(jnp.bfloat16)
    local_ids = lax.axis_index("exp") * EXP_DEV + jnp.arange(EXP_DEV)
    matches = expert_ids[None, :, :] == local_ids[:, None, None]
    is_named = jnp.any(matches, axis=2)
    gate_local = jnp.sum(jnp.where(matches, gate_values[None, :, :], 0.0), axis=2)
    slot_index = jnp.cumsum(is_named.astype(jnp.int32), axis=1) - 1
    placement = is_named[:, None, :] & (slot_index[:, None, :] == jnp.arange(CAP)[None, :, None])
    slot_gate = jnp.sum(jnp.where(placement, gate_local[:, None, :], 0.0), axis=2)
    slot_select = placement.astype(jnp.bfloat16)
    columns = slot_select
    packed = jnp.einsum(
        "kct,td->kcd",
        columns,
        lax.all_gather(normed, "exp", axis=0, tiled=True),
        preferred_element_type=jnp.float32,
    )
    packed = packed.astype(jnp.bfloat16)
    group_size = lax.axis_size("req") // EXP_DEV
    outbound = jnp.repeat(packed, group_size, axis=0)
    inner_weights = w_in[0, 0]
    outer_weights = w_out[0, 0]
    inbound = lax.all_to_all(outbound, "req", split_axis=0, concat_axis=0, tiled=True)
    hidden = jnp.einsum("scd,df->scf", inbound, inner_weights, preferred_element_type=jnp.float32)
    activated = jax.nn.silu(hidden).astype(jnp.bfloat16)
    returned = lax.all_to_all(
        jnp.einsum(
            "scf,fd->scd", activated, outer_weights, preferred_element_type=jnp.float32
        ).astype(jnp.bfloat16),
        "req",
        split_axis=0,
        concat_axis=0,
        tiled=True,
    )
    expert_out = jnp.sum(
        returned.reshape(EXP_DEV, group_size, CAP, model_width).astype(jnp.float32), axis=1
    )
    weighted = expert_out * slot_gate[:, :, None]
    slot_select_wide = placement.astype(jnp.float32)
    columns = slot_select_wide
    expert_mix = lax.psum_scatter(
        jnp.einsum("kct,kcd->td", columns, weighted, precision=lax.Precision.HIGHEST).astype(
            jnp.bfloat16
        ),
        "exp",
        scatter_dimension=0,
        tiled=True,
    ).astype(jnp.float32)
    return (residual + expert_mix).astype(jnp.bfloat16)


def solution(mesh):
    placed = (
        P(("req", "exp"), None),
        P(("req", "exp"), None),
        P(("req", "exp"), None),
        P("req", "exp", None, None, None),
        P(("req", "exp"), None),
        P(("req", "exp")),
        P("req", "exp", None, None),
        P("req", "exp", None, None),
        P("req", None),
        P("req", None),
        P(),
        P("exp", "req", None, None),
        P("exp", "req", None, None),
    )
    return jax.shard_map(
        body, mesh=mesh, in_specs=placed, out_specs=P(("req", "exp"), None), check_vma=False
    )
```

profile of v0, /device:TPU:2, one launch (start us, length us, event | category | flops | bytes accessed | tf_op | source)
XLA Modules:
  0.0 401.4 jit_solution(36043764672212285)
XLA Ops:
  6.5 0.0 copy-start
  6.5 0.0 copy-start.13
  6.6 0.0 copy-start.14
  6.6 0.0 copy-start.4
  6.6 1.4 copy.45
  7.9 0.0 copy-done.13
  8.0 0.6 gather_fusion
  8.5 3.4 collective-permute-start
  11.9 0.6 gather_fusion.1
  12.5 6.3 %collective-permute-start.1 = (bf16[4,16,1024]{2,1,0:T(8,128)(2,1)S(1)}, bf16[4,16,1024]{2,1,0:T(8,128)(2,1)S(1)}, u32[]{:S(2)}, u32[]{:S(2)}) collective-permute-start(bf16[4,16,1024]{2,1,0:T(8,128)(2,1)S(1)} %gather_fusion.1), channel_id=1, source_target_pairs={{16,0},{32,16},{48,32},{64,48},{80,64},{96,80},{112,96},{128,112},... | collective-permute-start | bytes 393224 | tf_op jit(solution)/shard_map/ppermute | solution.py:24
  18.8 0.0 copy-done.14
  18.9 0.0 copy-done.10
  18.9 0.1 reshape.250
  19.0 0.6 pad_clamp_fusion
  19.6 0.0 copy-done.15
  19.6 0.7 iota_compare_fusion.1
  20.2 0.0 copy-done.4
  20.2 0.1 compare_reduce_fusion
  20.3 0.4 copy-done.11
  20.7 0.3 reduce_window_sum.11
  21.0 0.2 copy-done.7
  21.2 0.6 fusion.31
  21.8 0.0 copy-done.6
  21.8 0.0 copy-done.3
  21.8 0.1 reshape.228
  21.9 1.3 convert_element_type.45
  23.2 0.7 broadcast_in_dim.77
  23.9 0.0 collective-permute-done
  23.9 0.0 collective-permute-done.1
  24.0 0.9 scatter_fusion
  24.9 1.7 gather_fusion.2
  26.6 1.3 pad_maximum_fusion
  27.9 0.2 reshape.227
  28.1 0.2 reshape.226
  28.3 0.0 copy-start.1
  28.3 0.0 copy-start.2
  28.3 0.5 fusion.36
  28.8 0.2 fusion.18
  29.0 0.0 copy-start.8
  29.0 0.6 fusion.7
  29.7 0.0 copy-done.1
  29.7 0.1 multiply_reduce_fusion
  29.9 0.0 copy-done.2
  29.9 0.1 multiply_convert_fusion.1
  30.0 21.8 %all_gather.3 = bf16[128,3584]{1,0:T(8,128)(2,1)S(1)} all-gather(bf16[8,3584]{1,0:T(8,128)(2,1)S(1)} %multiply_convert_fusion.1), channel_id=1, replica_groups=mesh['req'=32,'exp'=16] {'exp'}, dimensions={0}, use_global_device_ids=true | all-gather | bytes 974848 | tf_op jit(solution)/shard_map/all_gather | solution.py:115
  51.8 0.0 copy-done.8
  51.8 0.3 convolution_convert_fusion.1
  52.1 0.4 broadcast_in_dim.82
  52.5 135.6 %all_to_all.10 = bf16[32,24,3584]{2,1,0:T(8,128)(2,1)} all-to-all(bf16[32,24,3584]{2,1,0:T(8,128)(2,1)S(1)} %bitcast.52), channel_id=1, replica_groups=mesh['req'=32,'exp'=16] {'req'}, dimensions={0} | all-to-all | bytes 11010048 | tf_op jit(solution)/shard_map/all_to_all | solution.py:123
  188.1 0.0 copy-done
  188.1 11.5 %convolution_convert_fusion = bf16[32,24,3584]{2,1,0:T(8,128)(2,1)} fusion(bf16[1,1,256,3584]{3,2,1,0:T(8,128)(2,1)S(1)} %copy-done, bf16[32,24,3584]{2,1,0:T(8,128)(2,1)} %all_to_all.10, bf16[1,1,3584,256]{3,2,1,0:T(8,128)(2,1)} %param.24), kind=kOutput, calls=%fused_computation.5 | convolution fusion | flops 2822307840 | bytes 14680064 | tf_op jit(solution)/shard_map/scf,fd->scd/dot_general | solution.py:127
  199.6 6.3 %all-to-all-start.1 = ((bf16[32,24,3584]{2,1,0:T(8,128)(2,1)}), bf16[32,24,3584]{2,1,0:T(8,128)(2,1)}, u32[]{:S(2)}, u32[]{:S(2)}) async-start(bf16[32,24,3584]{2,1,0:T(8,128)(2,1)} %convolution_convert_fusion), calls=%async_computation.1 | async-start | bytes 11010048 | tf_op jit(solution)/shard_map/all_to_all | solution.py:126
  205.9 0.0 reduce-scatter.2.cloned.1.call-start
  206.0 0.0 copy-done.5
  206.0 0.0 copy-done.9
  206.0 0.0 copy-done.12
  206.0 0.1 fusion.30
  206.1 0.1 select_reduce_fusion
  206.2 125.1 %all-to-all-done.1 = bf16[32,24,3584]{2,1,0:T(8,128)(2,1)} async-done(((bf16[32,24,3584]{2,1,0:T(8,128)(2,1)}), bf16[32,24,3584]{2,1,0:T(8,128)(2,1)}, u32[]{:S(2)}, u32[]{:S(2)}) %all-to-all-start.1) | async-done | bytes 5505056 | tf_op jit(solution)/shard_map/all_to_all | solution.py:126
  331.3 3.5 convert_reduce_fusion
  334.8 2.0 fusion
  336.7 0.0 reduce-scatter.2.cloned.1.call-update
  336.8 56.4 %reduce-scatter.2.cloned.1.call-done = bf16[8,3584]{1,0:T(8,128)(2,1)} async-done(((bf16[128,3584]{1,0:T(8,128)(2,1)}), bf16[8,3584]{1,0:T(8,128)(2,1)}) %reduce-scatter.2.cloned.1.call-update) | async-done | bytes 57360 | tf_op jit(solution)/shard_map/reduce_scatter | solution.py:141
  393.1 1.5 add_convert_fusion
  (25 shorter events, 0.2 us)
Async XLA Ops:
  6.5 181.5 %copy-start = (bf16[1,1,256,3584]{3,2,1,0:T(8,128)(2,1)S(1)}, bf16[1,1,256,3584]{3,2,1,0:T(8,128)(2,1)}, u32[]{:S(2)}) copy-start(bf16[1,1,256,3584]{3,2,1,0:T(8,128)(2,1)} %param.25) | copy-start | bytes 5505028
  6.5 15.3 %copy-start.3 = (bf16[8,3584]{1,0:T(8,128)(2,1)S(1)}, bf16[8,3584]{1,0:T(8,128)(2,1)}, u32[]{:S(2)}) copy-start(bf16[8,3584]{1,0:T(8,128)(2,1)} %param.14) | copy-start | bytes 172036
  6.5 15.3 %copy-start.6 = (bf16[8,1024]{1,0:T(8,128)(2,1)S(1)}, bf16[8,1024]{1,0:T(8,128)(2,1)}, u32[]{:S(2)}) copy-start(bf16[8,1024]{1,0:T(8,128)(2,1)} %param.15) | copy-start | bytes 49156
  6.5 12.3 %copy-start.10 = (s32[4,8]{1,0:T(4,128)S(1)}, s32[4,8]{1,0:T(4,128)}, u32[]{:S(2)}) copy-start(s32[4,8]{1,0:T(4,128)} %param.17) | copy-start | bytes 388
  6.5 13.0 %copy-start.15 = (s32[4]{0:T(128)S(1)}, s32[4]{0:T(128)}, u32[]{:S(2)}) copy-start(s32[4]{0:T(128)} %param.18) | copy-start | bytes 52
  6.5 1.4 copy-start.13
  6.6 12.3 %copy-start.14 = (s32[1,1,2,4]{3,2,1,0:T(2,128)S(1)}, s32[1,1,2,4]{3,2,1,0:T(2,128)}, u32[]{:S(2)}) copy-start(s32[1,1,2,4]{3,2,1,0:T(2,128)} %param.20) | copy-start | bytes 100
  6.6 13.7 %copy-start.4 = (s32[128,8]{0,1:T(8,128)S(1)}, s32[128,8]{0,1:T(8,128)}, u32[]{:S(2)}) copy-start(s32[128,8]{0,1:T(8,128)} %param.21) | copy-start | bytes 12292
  8.5 15.4 %collective-permute-start = (bf16[4,16,1024]{2,1,0:T(8,128)(2,1)S(1)}, bf16[4,16,1024]{2,1,0:T(8,128)(2,1)S(1)}, u32[]{:S(2)}, u32[]{:S(2)}) collective-permute-start(bf16[4,16,1024]{2,1,0:T(8,128)(2,1)S(1)} %gather_fusion), channel_id=1, source_target_pairs={{0,16},{16,32},{32,48},{48,64},{64,80},{80,96},{96,112},{112,128},... | collective-permute-start | bytes 393224 | tf_op jit(solution)/shard_map/ppermute | solution.py:21
  12.5 11.4 %collective-permute-start.1 = (bf16[4,16,1024]{2,1,0:T(8,128)(2,1)S(1)}, bf16[4,16,1024]{2,1,0:T(8,128)(2,1)S(1)}, u32[]{:S(2)}, u32[]{:S(2)}) collective-permute-start(bf16[4,16,1024]{2,1,0:T(8,128)(2,1)S(1)} %gather_fusion.1), channel_id=1, source_target_pairs={{16,0},{32,16},{48,32},{64,48},{80,64},{96,80},{112,96},{128,112},... | collective-permute-start | bytes 393224 | tf_op jit(solution)/shard_map/ppermute | solution.py:24
  20.2 0.5 copy-start.11
  20.7 0.5 copy-start.7
  28.3 1.4 copy-start.1
  28.3 1.6 copy-start.2
  29.0 22.8 %copy-start.8 = (pred[4,128]{1,0:T(4,128)(4,1)S(1)}, pred[4,128]{1,0:T(4,128)(4,1)}, u32[]{:S(2)}) copy-start(pred[4,128]{1,0:T(4,128)(4,1)} %copy-done.7) | copy-start | bytes 1540
  199.6 6.4 %copy-start.5 = (s32[128,8]{0,1:T(8,128)S(1)}, s32[128,8]{0,1:T(8,128)}, u32[]{:S(2)}) copy-start(s32[128,8]{0,1:T(8,128)} %param.21) | copy-start | bytes 12292
  199.6 6.4 %copy-start.9 = (f32[128,8]{0,1:T(8,128)S(1)}, f32[128,8]{0,1:T(8,128)}, u32[]{:S(2)}) copy-start(f32[128,8]{0,1:T(8,128)} %param.22) | copy-start | bytes 12292
  199.6 6.4 %copy-start.12 = (s32[4]{0:T(128)S(1)}, s32[4]{0:T(128)}, u32[]{:S(2)}) copy-start(s32[4]{0:T(128)} %copy-done.11) | copy-start | bytes 52
  199.6 131.7 %all-to-all-start.1 = ((bf16[32,24,3584]{2,1,0:T(8,128)(2,1)}), bf16[32,24,3584]{2,1,0:T(8,128)(2,1)}, u32[]{:S(2)}, u32[]{:S(2)}) async-start(bf16[32,24,3584]{2,1,0:T(8,128)(2,1)} %convolution_convert_fusion), calls=%async_computation.1 | async-start | bytes 11010048 | tf_op jit(solution)/shard_map/all_to_all | solution.py:126
  205.9 187.2 %reduce-scatter.2.cloned.1.call-start = ((), (), s32[]{:S(2)}) async-start(), calls=%async_computation.3 | async-start | bytes 974848 | tf_op jit(solution)/shard_map/reduce_scatter | solution.py:141
Sparse Core Ops, SparseCore 0:
  336.9 56.1 reduce-scatter.1
where the time goes:
time: 402 us; the launch traced here: 401 us
  waiting for transfers between devices  182 us (45%)
  blocking collectives  157 us (39%)
  starting transfers between devices  16 us (4%)
  matrix products  14.9 us (4%)
  between operations  13.7 us (3%)
  other arithmetic  10.5 us (3%)
  local copies, waits for them, and re-layouts  7.34 us (2%)
    all_to_all x1, blocking collectives, body(): lax.all_to_all(outbound, 'req', split_axis=0, concat_axis=0, tiled=True)  136 us
    all_to_all x1, waiting for transfers between devices, body(): lax.all_to_all(jnp.einsum('scf,fd->scd', activated, outer_weights, prefer...  125 us
    reduce_scatter x1, waiting for transfers between devices, body(): lax.psum_scatter(jnp.einsum('kct,kcd->td', columns, weighted, precision=l...  56.4 us
    all_gather x1, blocking collectives, body(): lax.all_gather(normed, 'exp', axis=0, tiled=True)  21.8 us
    dot_general x1, matrix products, body(): jnp.einsum('scf,fd->scd', activated, outer_weights, preferred_element_typ...  11.5 us
  transfers between devices with their start and end apart: 4, of which 2 were waited for; matrix products, arithmetic and copies ran while one was open for 1% of the time, Pallas kernels for 0%

commit v1 on v0

--- a/solution.py
+++ b/solution.py
@@ -10,6 +10,13 @@
 CAP = 24
 neg_big = -1e30
 norm_eps = 1e-06
+
+
+def exchange_gather(x, name, d):
+    count = lax.axis_size(name)
+    blocks = jnp.stack([x for _ in range(count)])
+    blocks = lax.all_to_all(blocks, name, split_axis=0, concat_axis=0)
+    return jnp.concatenate(blocks, axis=d)
 
 
 def with_halo(block, sides, width):
@@ -112,7 +119,7 @@
     packed = jnp.einsum(
         "kct,td->kcd",
         columns,
-        lax.all_gather(normed, "exp", axis=0, tiled=True),
+        exchange_gather(normed, "exp", 0),
         preferred_element_type=jnp.float32,
     )
     packed = packed.astype(jnp.bfloat16)

time: 402 us -> 416 us (1.035)
  waiting for transfers between devices: 182 us -> 209 us
  blocking collectives: 157 us -> 136 us
  starting transfers between devices: 16 us -> 24.6 us
    all_to_all x0 -> x1, waiting for transfers between devices: none -> 22.7 us  [exchange_gather(): blocks = lax.all_to_all(blocks, name, split_axis=0, concat_axis=0)]
    all_gather x1 -> x0, blocking collectives: 21.8 us -> none  [body(): lax.all_gather(normed, 'exp', axis=0, tiled=True)]
    all_to_all x0 -> x1, starting transfers between devices: none -> 8.47 us  [exchange_gather(): blocks = lax.all_to_all(blocks, name, split_axis=0, concat_axis=0)]
  transfers between devices with their start and end apart: 4 -> 5, of which waited for: 2 -> 4; matrix products, arithmetic and copies ran while one was open for 1% -> 1% of each run, Pallas kernels for 0% -> 0%
where the time goes in v1:
time: 416 us
  waiting for transfers between devices  209 us (50%)
  blocking collectives  136 us (33%)
  starting transfers between devices  24.6 us (6%)
  matrix products  16.5 us (4%)
  between operations  13.7 us (3%)
  other arithmetic  8.81 us (2%)
  local copies, waits for them, and re-layouts  7.43 us (2%)
    all_to_all x1, blocking collectives, body(): lax.all_to_all(outbound, 'req', split_axis=0, concat_axis=0, tiled=True)  136 us
    all_to_all x1, waiting for transfers between devices, body(): lax.all_to_all(jnp.einsum('scf,fd->scd', activated, outer_weights, prefer...  128 us
    reduce_scatter x1, waiting for transfers between devices, body(): lax.psum_scatter(jnp.einsum('kct,kcd->td', columns, weighted, precision=l...  57.2 us
    all_to_all x1, waiting for transfers between devices, exchange_gather(): blocks = lax.all_to_all(blocks, name, split_axis=0, concat_axis=0)  22.7 us
    dot_general x1, matrix products, body(): jnp.einsum('scf,fd->scd', activated, outer_weights, preferred_element_typ...  11.5 us
    all_to_all x1, starting transfers between devices, exchange_gather(): blocks = lax.all_to_all(blocks, name, split_axis=0, concat_axis=0)  8.47 us
  transfers between devices with their start and end apart: 5, of which 4 were waited for; matrix products, arithmetic and copies ran while one was open for 1% of the time, Pallas kernels for 0%

profile of v1, /device:TPU:2, one launch (start us, length us, event | category | flops | bytes accessed | tf_op | source)
XLA Modules:
  0.0 415.8 jit_solution(5644534001552788848)
XLA Ops:
  6.5 0.0 copy-start
  6.5 0.0 copy-start.2
  6.5 0.0 copy-start.4
  6.5 0.0 copy-start.7
  6.5 0.0 copy-start.10
  6.5 0.0 copy-start.8
  6.6 0.0 copy-start.9
  6.6 0.0 copy-start.5
  6.6 1.4 copy.45
  7.9 0.0 copy-done.8
  7.9 0.6 gather_fusion
  8.5 3.4 collective-permute-start
  11.9 0.6 gather_fusion.1
  12.5 6.3 %collective-permute-start.1 = (bf16[4,16,1024]{2,1,0:T(8,128)(2,1)S(1)}, bf16[4,16,1024]{2,1,0:T(8,128)(2,1)S(1)}, u32[]{:S(2)}, u32[]{:S(2)}) collective-permute-start(bf16[4,16,1024]{2,1,0:T(8,128)(2,1)S(1)} %gather_fusion.1), channel_id=1, source_target_pairs={{16,0},{32,16},{48,32},{64,48},{80,64},{96,80},{112,96},{128,112},... | collective-permute-start | bytes 393224 | tf_op jit(solution)/shard_map/ppermute | solution.py:31
  18.8 0.0 copy-done.9
  18.8 0.0 copy-done.7
  18.9 0.1 reshape.256
  19.0 0.0 copy-done.10
  19.0 0.1 iota_compare_fusion.1
  19.0 0.1 fusion.31
  19.1 0.0 copy-done.4
  19.1 0.0 copy-done.2
  19.1 0.7 reshape.233
  19.9 0.0 copy-done.5
  19.9 0.6 pad_add_fusion
  20.5 0.0 collective-permute-done
  20.5 0.8 collective-permute-done.1
  21.3 0.8 scatter_fusion
  22.1 1.6 gather_fusion.2
  23.7 1.3 pad_maximum_fusion
  25.0 0.2 reshape.232
  25.2 0.2 reshape.231
  25.4 0.0 copy-start.1
  25.4 1.3 fusion.36
  26.8 0.9 fusion.18
  27.7 1.3 fusion.7
  29.0 0.0 copy-start.3
  29.0 0.0 copy-done.1
  29.0 0.1 multiply_reduce_fusion
  29.2 0.1 multiply_convert_fusion.1
  29.3 1.0 stack.2
  30.3 8.5 %all-to-all-start = ((bf16[16,8,3584]{2,1,0:T(8,128)(2,1)}), bf16[16,8,3584]{2,1,0:T(8,128)(2,1)S(1)}, u32[]{:S(2)}, u32[]{:S(2)}) async-start(bf16[16,8,3584]{2,1,0:T(8,128)(2,1)} %stack.2), calls=%async_computation | async-start | bytes 1835008 | tf_op jit(solution)/shard_map/all_to_all | solution.py:18
  38.8 0.0 copy-done.3
  38.8 0.1 compare_reduce_fusion
  38.9 0.3 reduce_window_sum.11
  39.2 22.7 %all-to-all-done = bf16[16,8,3584]{2,1,0:T(8,128)(2,1)S(1)} async-done(((bf16[16,8,3584]{2,1,0:T(8,128)(2,1)}), bf16[16,8,3584]{2,1,0:T(8,128)(2,1)S(1)}, u32[]{:S(2)}, u32[]{:S(2)}) %all-to-all-start) | async-done | bytes 917536 | tf_op jit(solution)/shard_map/all_to_all | solution.py:18
  61.9 0.3 convolution_convert_fusion.1
  62.2 0.4 broadcast_in_dim.82
  62.6 135.6 %all_to_all.15 = bf16[32,24,3584]{2,1,0:T(8,128)(2,1)} all-to-all(bf16[32,24,3584]{2,1,0:T(8,128)(2,1)S(1)} %bitcast.54), channel_id=1, replica_groups=mesh['req'=32,'exp'=16] {'req'}, dimensions={0} | all-to-all | bytes 11010048 | tf_op jit(solution)/shard_map/all_to_all | solution.py:130
  198.2 0.0 copy-done
  198.2 11.5 %convolution_convert_fusion = bf16[32,24,3584]{2,1,0:T(8,128)(2,1)} fusion(bf16[1,1,256,3584]{3,2,1,0:T(8,128)(2,1)S(1)} %copy-done, bf16[32,24,3584]{2,1,0:T(8,128)(2,1)} %all_to_all.15, bf16[1,1,3584,256]{3,2,1,0:T(8,128)(2,1)} %param.24), kind=kOutput, calls=%fused_computation.5 | convolution fusion | flops 2822307840 | bytes 14680064 | tf_op jit(solution)/shard_map/scf,fd->scd/dot_general | solution.py:134
  209.8 0.0 copy-start.6
  209.8 6.4 %all-to-all-start.2 = ((bf16[32,24,3584]{2,1,0:T(8,128)(2,1)}), bf16[32,24,3584]{2,1,0:T(8,128)(2,1)}, u32[]{:S(2)}, u32[]{:S(2)}) async-start(bf16[32,24,3584]{2,1,0:T(8,128)(2,1)} %convolution_convert_fusion), calls=%async_computation.2 | async-start | bytes 11010048 | tf_op jit(solution)/shard_map/all_to_all | solution.py:133
  216.1 0.0 reduce-scatter.2.cloned.1.call-start
  216.2 0.0 copy-done.6
  216.2 0.1 fusion.30
  216.3 0.1 select_reduce_fusion
  216.4 128.5 %all-to-all-done.2 = bf16[32,24,3584]{2,1,0:T(8,128)(2,1)} async-done(((bf16[32,24,3584]{2,1,0:T(8,128)(2,1)}), bf16[32,24,3584]{2,1,0:T(8,128)(2,1)}, u32[]{:S(2)}, u32[]{:S(2)}) %all-to-all-start.2) | async-done | bytes 5505056 | tf_op jit(solution)/shard_map/all_to_all | solution.py:133
  344.9 3.5 convert_reduce_fusion
  348.3 2.0 fusion
  350.3 0.0 reduce-scatter.2.cloned.1.call-update
  350.3 57.2 %reduce-scatter.2.cloned.1.call-done = bf16[8,3584]{1,0:T(8,128)(2,1)} async-done(((bf16[128,3584]{1,0:T(8,128)(2,1)}), bf16[8,3584]{1,0:T(8,128)(2,1)}) %reduce-scatter.2.cloned.1.call-update) | async-done | bytes 57360 | tf_op jit(solution)/shard_map/reduce_scatter | solution.py:148
  407.5 1.5 add_convert_fusion
  (18 shorter events, 0.2 us)
Async XLA Ops:
  6.5 191.7 %copy-start = (bf16[1,1,256,3584]{3,2,1,0:T(8,128)(2,1)S(1)}, bf16[1,1,256,3584]{3,2,1,0:T(8,128)(2,1)}, u32[]{:S(2)}) copy-start(bf16[1,1,256,3584]{3,2,1,0:T(8,128)(2,1)} %param.25) | copy-start | bytes 5505028
  6.5 12.6 %copy-start.2 = (bf16[8,3584]{1,0:T(8,128)(2,1)S(1)}, bf16[8,3584]{1,0:T(8,128)(2,1)}, u32[]{:S(2)}) copy-start(bf16[8,3584]{1,0:T(8,128)(2,1)} %param.14) | copy-start | bytes 172036
  6.5 12.6 %copy-start.4 = (bf16[8,1024]{1,0:T(8,128)(2,1)S(1)}, bf16[8,1024]{1,0:T(8,128)(2,1)}, u32[]{:S(2)}) copy-start(bf16[8,1024]{1,0:T(8,128)(2,1)} %param.15) | copy-start | bytes 49156
  6.5 12.3 %copy-start.7 = (s32[4,8]{1,0:T(4,128)S(1)}, s32[4,8]{1,0:T(4,128)}, u32[]{:S(2)}) copy-start(s32[4,8]{1,0:T(4,128)} %param.17) | copy-start | bytes 388
  6.5 12.4 %copy-start.10 = (s32[4]{0:T(128)S(1)}, s32[4]{0:T(128)}, u32[]{:S(2)}) copy-start(s32[4]{0:T(128)} %param.18) | copy-start | bytes 52
  6.5 1.4 copy-start.8
  6.6 12.3 %copy-start.9 = (s32[1,1,2,4]{3,2,1,0:T(2,128)S(1)}, s32[1,1,2,4]{3,2,1,0:T(2,128)}, u32[]{:S(2)}) copy-start(s32[1,1,2,4]{3,2,1,0:T(2,128)} %param.20) | copy-start | bytes 100
  6.6 13.3 %copy-start.5 = (bf16[3584]{0:T(1024)(128)(2,1)S(1)}, bf16[3584]{0:T(1024)(128)(2,1)}, u32[]{:S(2)}) copy-start(bf16[3584]{0:T(1024)(128)(2,1)} %param.23) | copy-start | bytes 21508
  8.5 12.0 %collective-permute-start = (bf16[4,16,1024]{2,1,0:T(8,128)(2,1)S(1)}, bf16[4,16,1024]{2,1,0:T(8,128)(2,1)S(1)}, u32[]{:S(2)}, u32[]{:S(2)}) collective-permute-start(bf16[4,16,1024]{2,1,0:T(8,128)(2,1)S(1)} %gather_fusion), channel_id=1, source_target_pairs={{0,16},{16,32},{32,48},{48,64},{64,80},{80,96},{96,112},{112,128},... | collective-permute-start | bytes 393224 | tf_op jit(solution)/shard_map/ppermute | solution.py:28
  12.5 8.8 %collective-permute-start.1 = (bf16[4,16,1024]{2,1,0:T(8,128)(2,1)S(1)}, bf16[4,16,1024]{2,1,0:T(8,128)(2,1)S(1)}, u32[]{:S(2)}, u32[]{:S(2)}) collective-permute-start(bf16[4,16,1024]{2,1,0:T(8,128)(2,1)S(1)} %gather_fusion.1), channel_id=1, source_target_pairs={{16,0},{32,16},{48,32},{64,48},{80,64},{96,80},{112,96},{128,112},... | collective-permute-start | bytes 393224 | tf_op jit(solution)/shard_map/ppermute | solution.py:31
  25.4 3.7 copy-start.1
  29.0 9.8 %copy-start.3 = (s32[128,8]{0,1:T(8,128)S(1)}, s32[128,8]{0,1:T(8,128)}, u32[]{:S(2)}) copy-start(s32[128,8]{0,1:T(8,128)} %param.21) | copy-start | bytes 12292
  30.3 31.6 %all-to-all-start = ((bf16[16,8,3584]{2,1,0:T(8,128)(2,1)}), bf16[16,8,3584]{2,1,0:T(8,128)(2,1)S(1)}, u32[]{:S(2)}, u32[]{:S(2)}) async-start(bf16[16,8,3584]{2,1,0:T(8,128)(2,1)} %stack.2), calls=%async_computation | async-start | bytes 1835008 | tf_op jit(solution)/shard_map/all_to_all | solution.py:18
  209.8 6.4 %copy-start.6 = (f32[128,8]{0,1:T(8,128)S(1)}, f32[128,8]{0,1:T(8,128)}, u32[]{:S(2)}) copy-start(f32[128,8]{0,1:T(8,128)} %param.22) | copy-start | bytes 12292
  209.8 135.1 %all-to-all-start.2 = ((bf16[32,24,3584]{2,1,0:T(8,128)(2,1)}), bf16[32,24,3584]{2,1,0:T(8,128)(2,1)}, u32[]{:S(2)}, u32[]{:S(2)}) async-start(bf16[32,24,3584]{2,1,0:T(8,128)(2,1)} %convolution_convert_fusion), calls=%async_computation.2 | async-start | bytes 11010048 | tf_op jit(solution)/shard_map/all_to_all | solution.py:133
  216.1 191.4 %reduce-scatter.2.cloned.1.call-start = ((), (), s32[]{:S(2)}) async-start(), calls=%async_computation.4 | async-start | bytes 974848 | tf_op jit(solution)/shard_map/reduce_scatter | solution.py:148
Sparse Core Ops, SparseCore 0:
  350.4 57.0 reduce-scatter.1
